TPU v7x, 32 devices: a whole 2x2x4 slice. The times are simulated.
32 devices in a mesh: row: 8 (over z, core), col: 4 (over y, x).
Axes of the slice: x: 2, y: 2, z: 4, core: 2. Of those that a mesh axis runs over, the one named last changes fastest.
Arguments:
- gram: bfloat16 [32768, 32768], P('row', 'col'), may hold values from -1 to 5, as said below
- start_basis: bfloat16 [32768, 256], P(('row', 'col')), may hold values from -12 to 12
- slab: float32 [32768, 4096], P('row', 'col'), may hold values from -6 to 6
Outputs:
- core_scaled: float32 [32768, 256], P(('row', 'col'))
- next_unfolding: float32 [4096, 256], P(('row', 'col'))
Inputs may be any that keep to these rules, and one draw needn't show every extreme that they name: gram is symmetric: entry (i, j) equals entry (j, i).
All inputs are finite; a program needn't handle non-finite values.
Results may differ from a plain program's by a relative error of at most 0.003.
Values may be sent and summed in bfloat16 or wider, within the bound.
A program may use at most 192 MiB of HBM per device.

v0:
```python
import math
import jax
import jax.numpy as jnp
from jax import lax
from jax.sharding import PartitionSpec as P

N = 32768
NMODE = 16


def body(gram, start_basis, slab):
    col_count = lax.axis_size("col")
    highest = lax.Precision.HIGHEST
    contract_rows = (((0,), (0,)), ((), ()))
    own_rows = lax.all_gather(start_basis, "col", axis=0, tiled=True)
    first_image = lax.psum_scatter(
        lax.dot_general(gram, own_rows, contract_rows, preferred_element_type=jnp.float32),
        "row",
        scatter_dimension=0,
        tiled=True,
    ).astype(jnp.bfloat16)
    col_rows = lax.all_gather(first_image, "row", axis=0, tiled=True)
    second_image = lax.psum_scatter(
        jnp.dot(gram, col_rows, preferred_element_type=jnp.float32),
        "col",
        scatter_dimension=0,
        tiled=True,
    )
    own_gram = lax.dot_general(
        second_image,
        second_image,
        contract_rows,
        precision=highest,
        preferred_element_type=jnp.float32,
    )
    small_gram = lax.psum(own_gram, ("row", "col"))
    factor = jnp.linalg.cholesky(small_gram)
    basis_cols = jax.scipy.linalg.solve_triangular(factor, second_image.T, lower=True).T
    block_basis = lax.all_gather(basis_cols, "col", axis=0, tiled=True)
    own_proj = lax.psum_scatter(
        lax.dot_general(
            block_basis, slab, contract_rows, precision=highest, preferred_element_type=jnp.float32
        ),
        "row",
        scatter_dimension=0,
        tiled=True,
    )
    core_out = basis_cols * math.sqrt(N)
    mode_share = NMODE // col_count
    grouped = own_proj.reshape(own_proj.shape[0], mode_share, own_proj.shape[1] // mode_share)
    regrouped = lax.all_to_all(grouped, "col", split_axis=0, concat_axis=1, tiled=True)
    return (
        core_out,
        regrouped.reshape(regrouped.shape[0] * regrouped.shape[1], regrouped.shape[2]),
    )


def solution(mesh):
    in_specs = (P("row", "col"), P(("row", "col"), None), P("row", "col"))
    out_specs = (P(("row", "col"), None), P(("row", "col"), None))
    return jax.shard_map(body, mesh=mesh, in_specs=in_specs, out_specs=out_specs, check_vma=False)
```

profile of v0, /device:TPU:0, one launch (start us, length us, event | category | flops | bytes accessed | tf_op | source)
XLA Modules:
  0.0 614.0 jit_solution(10611750755675535246)
XLA Ops:
  7.2 0.0 all-gather.4.cloned.1.call-start
  7.2 0.7 all-gather.4.cloned.1.call-update
  7.9 0.0 reduce-scatter.4.cloned.1.call-start
  7.9 39.8 %all-gather.4.cloned.1.call-done = bf16[4096,256]{1,0:T(8,128)(2,1)} async-done(((bf16[1024,256]{1,0:T(8,128)(2,1)}), bf16[4096,256]{1,0:T(8,128)(2,1)}) %all-gather.4.cloned.1.call-update) | async-done | bytes 2097168 | tf_op jit(solution)/shard_map/all_gather | solution.py:15
  47.8 30.0 %fusion.9 = f32[8192,256]{1,0:T(8,128)} fusion(bf16[4096,8192]{1,0:T(8,128)(2,1)} %param.3, bf16[4096,256]{1,0:T(8,128)(2,1)} %all-gather.4.cloned.1.call-done), kind=kOutput, calls=%fused_computation.32 | convolution fusion | flops 17179869184 | bytes 77594624 | tf_op jit(solution)/shard_map/dot_general | solution.py:17
  77.7 0.0 reduce-scatter.4.cloned.1.call-update
  77.7 0.0 all-gather.6.cloned.1.call-start
  77.8 89.6 %reduce-scatter.4.cloned.1.call-done = f32[1024,256]{1,0:T(8,128)} async-done(((f32[8192,256]{1,0:T(8,128)}), f32[1024,256]{1,0:T(8,128)}) %reduce-scatter.4.cloned.1.call-update) | async-done | bytes 1048592 | tf_op jit(solution)/shard_map/reduce_scatter | solution.py:16
  167.4 2.1 convert_element_type.3
  169.5 0.0 reduce-scatter.6.cloned.1.call-start
  169.6 45.4 %all-gather.6.cloned.1.call-done = bf16[8192,256]{1,0:T(8,128)(2,1)} async-done(((bf16[1024,256]{1,0:T(8,128)(2,1)}), bf16[8192,256]{1,0:T(8,128)(2,1)}) %all-gather.6.cloned.1.call-update) | async-done | bytes 4194320 | tf_op jit(solution)/shard_map/all_gather | solution.py:22
  215.0 29.2 %convolution_bitcast_fusion = f32[4096,256]{0,1:T(8,128)} fusion(bf16[8192,256]{1,0:T(8,128)(2,1)} %all-gather.6.cloned.1.call-done, bf16[4096,8192]{1,0:T(8,128)(2,1)} %param.3), kind=kOutput, calls=%fused_computation.2 | convolution fusion | flops 17179869184 | bytes 75497472 | tf_op jit(solution)/shard_map/dot_general | solution.py:24
  244.2 0.0 reduce-scatter.6.cloned.1.call-update
  244.2 0.0 all-reduce.3.cloned.1.call-start
  244.3 51.5 %reduce-scatter.6.cloned.1.call-done = f32[1024,256]{0,1:T(8,128)} async-done(((f32[4096,256]{0,1:T(8,128)}), f32[1024,256]{0,1:T(8,128)}) %reduce-scatter.6.cloned.1.call-update) | async-done | bytes 1048592 | tf_op jit(solution)/shard_map/reduce_scatter | solution.py:23
  295.8 3.4 fusion.10
  299.1 0.2 all-gather.8.cloned.1.call-start
  299.4 128.9 %all-reduce.3.cloned.1.call-done = f32[256,256]{0,1:T(8,128)} async-done(((f32[256,256]{0,1:T(8,128)}), f32[256,256]{0,1:T(8,128)}) %all-reduce.3.cloned.1.call-update) | async-done | bytes 262160 | tf_op jit(solution)/shard_map/psum | solution.py:36
  428.3 1.1 copy.6
  429.4 1.0 fusion.2
  430.4 11.7 %cholesky.50 = f32[128,128]{1,0:T(8,128)S(1)} custom-call(f32[128,128]{1,0:T(8,128)S(1)} %cholesky.118), custom_call_target="Cholesky" | custom-call | tf_op jit(solution)/shard_map/jit(cholesky)/cholesky | solution.py:37
  442.1 9.8 %custom-call.15 = f32[1,128,128]{1,2,0:T(8,128)S(1)} custom-call(f32[1,128,128]{2,1,0:T(8,128)S(1)} %get-tuple-element.25), custom_call_target="InvertDiagBlocksLowerTriangular" | custom-call | tf_op jit(solution)/shard_map/jit(cholesky)/cholesky | solution.py:37
  452.0 0.2 constant_dynamic-update-slice_fusion.1
  452.2 0.3 convolution_subtract_fusion.1
  452.4 11.7 %cholesky.105 = f32[128,128]{1,0:T(8,128)S(1)} custom-call(f32[128,128]{1,0:T(8,128)S(1)} %convolution_subtract_fusion.1), custom_call_target="Cholesky" | custom-call | tf_op jit(solution)/shard_map/jit(cholesky)/cholesky | solution.py:37
  464.2 0.7 compare_reduce_fusion
  466.3 0.1 triangular_solve.57
  466.4 4.3 while.1
  466.6 0.6 fusion.25
  467.1 1.4 bitcast_dynamic-update-slice_fusion.2
  468.6 0.6 fusion.25
  469.2 1.4 bitcast_dynamic-update-slice_fusion.2
  470.6 19.7 %custom-call.16 = f32[2,128,128]{1,2,0:T(8,128)S(1)} custom-call(f32[2,128,128]{2,1,0:T(8,128)S(1)} %get-tuple-element.9), custom_call_target="InvertDiagBlocksLowerTriangular" | custom-call | tf_op jit(solution)/shard_map/jit(_solve_triangular)/triangular_solve | solution.py:38
  490.3 0.6 fusion
  491.0 0.6 convolution_subtract_fusion
  491.6 0.6 fusion.4
  492.2 1.0 maximum_bitcast_fusion
  493.2 0.0 all-gather.8.cloned.1.call-update
  493.3 0.0 reduce-scatter.8.cloned.1.call-start
  493.3 51.7 %all-gather.8.cloned.1.call-done = f32[4096,256]{0,1:T(8,128)} async-done(((f32[1024,256]{0,1:T(8,128)}), f32[4096,256]{0,1:T(8,128)}) %all-gather.8.cloned.1.call-update) | async-done | bytes 4194320 | tf_op jit(solution)/shard_map/all_gather | solution.py:39
  545.1 18.3 %fusion.11 = f32[256,1024]{1,0:T(8,128)} fusion(f32[4096,256]{0,1:T(8,128)} %all-gather.8.cloned.1.call-done, f32[4096,1024]{1,0:T(8,128)} %param.5), kind=kOutput, calls=%fused_computation.34 | convolution fusion | flops 12884901888 | bytes 22020096 | tf_op jit(solution)/shard_map/dot_general | solution.py:41
  563.3 32.8 %reduce-scatter.8.cloned.1.call-done = f32[32,1024]{1,0:T(8,128)} async-done(((f32[256,1024]{1,0:T(8,128)}), f32[32,1024]{1,0:T(8,128)}) %reduce-scatter.8.cloned.1.call-update) | async-done | bytes 131088 | tf_op jit(solution)/shard_map/reduce_scatter | solution.py:40
  596.1 1.6 reshape.30
  597.7 3.7 all-to-all-start
  601.4 0.1 broadcast_multiply_fusion
  601.5 1.3 copy.8
  602.9 3.6 all-to-all-done
  606.4 0.7 reshape.31
  (15 shorter events, 0.2 us)
Async XLA Ops:
  7.2 40.6 %all-gather.4.cloned.1.call-start = ((), (), s32[]{:S(2)}) async-start(), calls=%async_computation.4 | async-start | bytes 2621440 | tf_op jit(solution)/shard_map/all_gather | solution.py:15
  7.9 159.5 %reduce-scatter.4.cloned.1.call-start = ((), (), s32[]{:S(2)}) async-start(), calls=%async_computation.5 | async-start | bytes 9437184 | tf_op jit(solution)/shard_map/reduce_scatter | solution.py:16
  77.7 137.3 %all-gather.6.cloned.1.call-start = ((), (), s32[]{:S(2)}) async-start(), calls=%async_computation.6 | async-start | bytes 4718592 | tf_op jit(solution)/shard_map/all_gather | solution.py:22
  169.5 126.2 %reduce-scatter.6.cloned.1.call-start = ((), (), s32[]{:S(2)}) async-start(), calls=%async_computation.7 | async-start | bytes 5242880 | tf_op jit(solution)/shard_map/reduce_scatter | solution.py:23
  244.2 184.1 %all-reduce.3.cloned.1.call-start = ((), (), s32[]{:S(2)}) async-start(), calls=%async_computation.8 | async-start | bytes 524288 | tf_op jit(solution)/shard_map/psum | solution.py:36
  295.8 194.6 %copy-start = (f32[1024,256]{0,1:T(8,128)S(1)}, f32[1024,256]{0,1:T(8,128)}, u32[]{:S(2)}) copy-start(f32[1024,256]{0,1:T(8,128)} %reduce-scatter.6.cloned.1.call-done) | copy-start | bytes 3145732
  299.1 245.9 %all-gather.8.cloned.1.call-start = ((), (), s32[]{:S(2)}) async-start(), calls=%async_computation.9 | async-start | bytes 5242880 | tf_op jit(solution)/shard_map/all_gather | solution.py:39
  493.3 102.9 %reduce-scatter.8.cloned.1.call-start = ((), (), s32[]{:S(2)}) async-start(), calls=%async_computation.10 | async-start | bytes 1179648 | tf_op jit(solution)/shard_map/reduce_scatter | solution.py:40
  597.7 8.7 %all-to-all-start = ((f32[32,4,256]{2,1,0:T(4,128)}), f32[32,4,256]{2,1,0:T(4,128)S(1)}, u32[]{:S(2)}, u32[]{:S(2)}) async-start(f32[32,4,256]{2,1,0:T(4,128)} %reshape.30), calls=%async_computation.3 | async-start | bytes 262144 | tf_op jit(solution)/shard_map/all_to_all | solution.py:51
Sparse Core Ops, SparseCore 0:
  9.8 37.8 all-gather.3
  77.9 89.5 reduce-scatter.3
  169.6 45.3 all-gather.5
  244.3 51.3 reduce-scatter.5
  301.7 126.5 all-reduce.2
  493.4 51.6 all-gather.7
  563.5 32.6 reduce-scatter.7
where the time goes:
time: 614 us
  waiting for transfers between devices  444 us (72%)
  matrix products  83.1 us (14%)
  other arithmetic  58 us (9%)
  between operations  15.6 us (3%)
  local copies, waits for them, and re-layouts  8.87 us (1%)
    psum x1, waiting for transfers between devices, body(): small_gram = lax.psum(own_gram, ('row', 'col'))  129 us
    reduce_scatter x1, waiting for transfers between devices, body(): lax.psum_scatter(lax.dot_general(gram, own_rows, contract_rows, preferred...  89.6 us
    all_gather x1, waiting for transfers between devices, body(): block_basis = lax.all_gather(basis_cols, 'col', axis=0, tiled=True)  51.7 us
    reduce_scatter x1, waiting for transfers between devices, body(): lax.psum_scatter(jnp.dot(gram, col_rows, preferred_element_type=jnp.float...  51.5 us
    all_gather x1, waiting for transfers between devices, body(): col_rows = lax.all_gather(first_image, 'row', axis=0, tiled=True)  45.4 us
    all_gather x1, waiting for transfers between devices, body(): own_rows = lax.all_gather(start_basis, 'col', axis=0, tiled=True)  39.8 us
    another operation x6, other arithmetic, body(): factor = jnp.linalg.cholesky(small_gram)  34 us
    reduce_scatter x1, waiting for transfers between devices, body(): lax.psum_scatter(lax.dot_general(block_basis, slab, contract_rows, precis...  32.8 us
  transfers between devices with their start and end apart: 8, of which 8 were waited for; matrix products, arithmetic and copies ran while one was open for 0% of the time, Pallas kernels for 0%

commit v1 on v0

--- a/solution.py
+++ b/solution.py
@@ -33,7 +33,7 @@
         precision=highest,
         preferred_element_type=jnp.float32,
     )
-    small_gram = lax.psum(own_gram, ("row", "col"))
+    small_gram = lax.psum(lax.psum(own_gram, "col"), "row")
     factor = jnp.linalg.cholesky(small_gram)
     basis_cols = jax.scipy.linalg.solve_triangular(factor, second_image.T, lower=True).T
     block_basis = lax.all_gather(basis_cols, "col", axis=0, tiled=True)

time: 614 us -> 586 us (0.954)
  waiting for transfers between devices: 444 us -> 416 us
    psum x1 -> x2, waiting for transfers between devices: 129 us -> 101 us  [body(): small_gram = lax.psum(lax.psum(own_gram, 'col'), 'row')]
  transfers between devices with their start and end apart: 8 -> 9, of which waited for: 8 -> 9; matrix products, arithmetic and copies ran while one was open for 0% -> 0% of each run, Pallas kernels for 0% -> 0%
where the time goes in v1:
time: 586 us
  waiting for transfers between devices  416 us (71%)
  matrix products  83.1 us (14%)
  other arithmetic  58 us (10%)
  between operations  15.6 us (3%)
  local copies, waits for them, and re-layouts  8.87 us (2%)
    psum x2, waiting for transfers between devices, body(): small_gram = lax.psum(lax.psum(own_gram, 'col'), 'row')  101 us
    reduce_scatter x1, waiting for transfers between devices, body(): lax.psum_scatter(lax.dot_general(gram, own_rows, contract_rows, preferred...  89.6 us
    all_gather x1, waiting for transfers between devices, body(): block_basis = lax.all_gather(basis_cols, 'col', axis=0, tiled=True)  51.7 us
    reduce_scatter x1, waiting for transfers between devices, body(): lax.psum_scatter(jnp.dot(gram, col_rows, preferred_element_type=jnp.float...  51.5 us
    all_gather x1, waiting for transfers between devices, body(): col_rows = lax.all_gather(first_image, 'row', axis=0, tiled=True)  45.4 us
    all_gather x1, waiting for transfers between devices, body(): own_rows = lax.all_gather(start_basis, 'col', axis=0, tiled=True)  39.8 us
    another operation x6, other arithmetic, body(): factor = jnp.linalg.cholesky(small_gram)  34 us
    reduce_scatter x1, waiting for transfers between devices, body(): lax.psum_scatter(lax.dot_general(block_basis, slab, contract_rows, precis...  32.8 us
  transfers between devices with their start and end apart: 9, of which 9 were waited for; matrix products, arithmetic and copies ran while one was open for 0% of the time, Pallas kernels for 0%

profile of v1, /device:TPU:0, one launch (start us, length us, event | category | flops | bytes accessed | tf_op | source)
XLA Modules:
  0.0 585.6 jit_solution(12584499165185488492)
XLA Ops:
  7.2 0.0 all-gather.4.cloned.1.call-start
  7.2 0.7 all-gather.4.cloned.1.call-update
  7.9 0.0 reduce-scatter.4.cloned.1.call-start
  7.9 39.8 %all-gather.4.cloned.1.call-done = bf16[4096,256]{1,0:T(8,128)(2,1)} async-done(((bf16[1024,256]{1,0:T(8,128)(2,1)}), bf16[4096,256]{1,0:T(8,128)(2,1)}) %all-gather.4.cloned.1.call-update) | async-done | bytes 2097168 | tf_op jit(solution)/shard_map/all_gather | solution.py:15
  47.8 30.0 %fusion.9 = f32[8192,256]{1,0:T(8,128)} fusion(bf16[4096,8192]{1,0:T(8,128)(2,1)} %param.3, bf16[4096,256]{1,0:T(8,128)(2,1)} %all-gather.4.cloned.1.call-done), kind=kOutput, calls=%fused_computation.32 | convolution fusion | flops 17179869184 | bytes 77594624 | tf_op jit(solution)/shard_map/dot_general | solution.py:17
  77.7 0.0 reduce-scatter.4.cloned.1.call-update
  77.7 0.0 all-gather.6.cloned.1.call-start
  77.8 89.6 %reduce-scatter.4.cloned.1.call-done = f32[1024,256]{1,0:T(8,128)} async-done(((f32[8192,256]{1,0:T(8,128)}), f32[1024,256]{1,0:T(8,128)}) %reduce-scatter.4.cloned.1.call-update) | async-done | bytes 1048592 | tf_op jit(solution)/shard_map/reduce_scatter | solution.py:16
  167.4 2.1 convert_element_type.3
  169.5 0.0 reduce-scatter.6.cloned.1.call-start
  169.6 45.4 %all-gather.6.cloned.1.call-done = bf16[8192,256]{1,0:T(8,128)(2,1)} async-done(((bf16[1024,256]{1,0:T(8,128)(2,1)}), bf16[8192,256]{1,0:T(8,128)(2,1)}) %all-gather.6.cloned.1.call-update) | async-done | bytes 4194320 | tf_op jit(solution)/shard_map/all_gather | solution.py:22
  215.0 29.2 %convolution_bitcast_fusion = f32[4096,256]{0,1:T(8,128)} fusion(bf16[8192,256]{1,0:T(8,128)(2,1)} %all-gather.6.cloned.1.call-done, bf16[4096,8192]{1,0:T(8,128)(2,1)} %param.3), kind=kOutput, calls=%fused_computation.2 | convolution fusion | flops 17179869184 | bytes 75497472 | tf_op jit(solution)/shard_map/dot_general | solution.py:24
  244.2 0.0 all-reduce.4.cloned.1.call-start
  244.3 51.5 %reduce-scatter.6.cloned.1.call-done = f32[1024,256]{0,1:T(8,128)} async-done(((f32[4096,256]{0,1:T(8,128)}), f32[1024,256]{0,1:T(8,128)}) %reduce-scatter.6.cloned.1.call-update) | async-done | bytes 1048592 | tf_op jit(solution)/shard_map/reduce_scatter | solution.py:23
  295.8 3.4 fusion.10
  299.1 0.0 all-reduce.6.cloned.1.call-start
  299.2 43.2 %all-reduce.4.cloned.1.call-done = f32[256,256]{0,1:T(8,128)} async-done(((f32[256,256]{0,1:T(8,128)}), f32[256,256]{0,1:T(8,128)}) %all-reduce.4.cloned.1.call-update) | async-done | bytes 262160 | tf_op jit(solution)/shard_map/psum | solution.py:36
  342.4 0.2 all-gather.8.cloned.1.call-start
  342.6 57.3 %all-reduce.6.cloned.1.call-done = f32[256,256]{0,1:T(8,128)} async-done(((f32[256,256]{0,1:T(8,128)}), f32[256,256]{0,1:T(8,128)}) %all-reduce.6.cloned.1.call-update) | async-done | bytes 262160 | tf_op jit(solution)/shard_map/psum | solution.py:36
  400.0 1.1 copy.6
  401.1 1.0 fusion.2
  402.1 11.7 %cholesky.50 = f32[128,128]{1,0:T(8,128)S(1)} custom-call(f32[128,128]{1,0:T(8,128)S(1)} %cholesky.118), custom_call_target="Cholesky" | custom-call | tf_op jit(solution)/shard_map/jit(cholesky)/cholesky | solution.py:37
  413.8 9.8 %custom-call.15 = f32[1,128,128]{1,2,0:T(8,128)S(1)} custom-call(f32[1,128,128]{2,1,0:T(8,128)S(1)} %get-tuple-element.25), custom_call_target="InvertDiagBlocksLowerTriangular" | custom-call | tf_op jit(solution)/shard_map/jit(cholesky)/cholesky | solution.py:37
  423.7 0.2 constant_dynamic-update-slice_fusion.1
  423.9 0.3 convolution_subtract_fusion.1
  424.2 11.7 %cholesky.105 = f32[128,128]{1,0:T(8,128)S(1)} custom-call(f32[128,128]{1,0:T(8,128)S(1)} %convolution_subtract_fusion.1), custom_call_target="Cholesky" | custom-call | tf_op jit(solution)/shard_map/jit(cholesky)/cholesky | solution.py:37
  435.9 0.7 compare_reduce_fusion
  438.0 0.1 triangular_solve.57
  438.1 4.3 while.1
  438.3 0.6 fusion.25
  438.9 1.4 bitcast_dynamic-update-slice_fusion.2
  440.3 0.6 fusion.25
  440.9 1.4 bitcast_dynamic-update-slice_fusion.2
  442.4 19.7 %custom-call.16 = f32[2,128,128]{1,2,0:T(8,128)S(1)} custom-call(f32[2,128,128]{2,1,0:T(8,128)S(1)} %get-tuple-element.9), custom_call_target="InvertDiagBlocksLowerTriangular" | custom-call | tf_op jit(solution)/shard_map/jit(_solve_triangular)/triangular_solve | solution.py:38
  462.1 0.6 fusion
  462.7 0.6 convolution_subtract_fusion
  463.3 0.6 fusion.4
  463.9 1.0 maximum_bitcast_fusion
  465.0 0.0 reduce-scatter.8.cloned.1.call-start
  465.0 51.7 %all-gather.8.cloned.1.call-done = f32[4096,256]{0,1:T(8,128)} async-done(((f32[1024,256]{0,1:T(8,128)}), f32[4096,256]{0,1:T(8,128)}) %all-gather.8.cloned.1.call-update) | async-done | bytes 4194320 | tf_op jit(solution)/shard_map/all_gather | solution.py:39
  516.8 18.3 %fusion.11 = f32[256,1024]{1,0:T(8,128)} fusion(f32[4096,256]{0,1:T(8,128)} %all-gather.8.cloned.1.call-done, f32[4096,1024]{1,0:T(8,128)} %param.5), kind=kOutput, calls=%fused_computation.34 | convolution fusion | flops 12884901888 | bytes 22020096 | tf_op jit(solution)/shard_map/dot_general | solution.py:41
  535.1 32.8 %reduce-scatter.8.cloned.1.call-done = f32[32,1024]{1,0:T(8,128)} async-done(((f32[256,1024]{1,0:T(8,128)}), f32[32,1024]{1,0:T(8,128)}) %reduce-scatter.8.cloned.1.call-update) | async-done | bytes 131088 | tf_op jit(solution)/shard_map/reduce_scatter | solution.py:40
  567.8 1.6 reshape.30
  569.5 3.6 all-to-all-start
  573.0 0.1 broadcast_multiply_fusion
  573.2 1.3 copy.8
  574.5 3.6 all-to-all-done
  578.1 0.7 reshape.31
  (18 shorter events, 0.3 us)
Async XLA Ops:
  7.2 40.6 %all-gather.4.cloned.1.call-start = ((), (), s32[]{:S(2)}) async-start(), calls=%async_computation.4 | async-start | bytes 2621440 | tf_op jit(solution)/shard_map/all_gather | solution.py:15
  7.9 159.5 %reduce-scatter.4.cloned.1.call-start = ((), (), s32[]{:S(2)}) async-start(), calls=%async_computation.5 | async-start | bytes 9437184 | tf_op jit(solution)/shard_map/reduce_scatter | solution.py:16
  77.7 137.3 %all-gather.6.cloned.1.call-start = ((), (), s32[]{:S(2)}) async-start(), calls=%async_computation.6 | async-start | bytes 4718592 | tf_op jit(solution)/shard_map/all_gather | solution.py:22
  169.5 126.2 %reduce-scatter.6.cloned.1.call-start = ((), (), s32[]{:S(2)}) async-start(), calls=%async_computation.7 | async-start | bytes 5242880 | tf_op jit(solution)/shard_map/reduce_scatter | solution.py:23
  244.2 98.2 %all-reduce.4.cloned.1.call-start = ((), (), s32[]{:S(2)}) async-start(), calls=%async_computation.8 | async-start | bytes 524288 | tf_op jit(solution)/shard_map/psum | solution.py:36
  295.8 166.3 %copy-start = (f32[1024,256]{0,1:T(8,128)S(1)}, f32[1024,256]{0,1:T(8,128)}, u32[]{:S(2)}) copy-start(f32[1024,256]{0,1:T(8,128)} %reduce-scatter.6.cloned.1.call-done) | copy-start | bytes 3145732
  299.1 100.8 %all-reduce.6.cloned.1.call-start = ((), (), s32[]{:S(2)}) async-start(), calls=%async_computation.9 | async-start | bytes 524288 | tf_op jit(solution)/shard_map/psum | solution.py:36
  342.4 174.4 %all-gather.8.cloned.1.call-start = ((), (), s32[]{:S(2)}) async-start(), calls=%async_computation.10 | async-start | bytes 5242880 | tf_op jit(solution)/shard_map/all_gather | solution.py:39
  465.0 102.9 %reduce-scatter.8.cloned.1.call-start = ((), (), s32[]{:S(2)}) async-start(), calls=%async_computation.11 | async-start | bytes 1179648 | tf_op jit(solution)/shard_map/reduce_scatter | solution.py:40
  569.5 8.6 %all-to-all-start = ((f32[32,4,256]{2,1,0:T(4,128)}), f32[32,4,256]{2,1,0:T(4,128)S(1)}, u32[]{:S(2)}, u32[]{:S(2)}) async-start(f32[32,4,256]{2,1,0:T(4,128)} %reshape.30), calls=%async_computation.3 | async-start | bytes 262144 | tf_op jit(solution)/shard_map/all_to_all | solution.py:51
Sparse Core Ops, SparseCore 0:
  9.8 37.8 all-gather.3
  77.9 89.5 reduce-scatter.3
  169.6 45.3 all-gather.5
  244.3 51.3 reduce-scatter.5
  299.3 43.0 all-reduce.3
  344.5 55.4 all-reduce.5
  465.1 51.6 all-gather.7
  535.2 32.6 reduce-scatter.7
